TPU v7x, 32 devices: a whole 2x2x4 slice. The times are simulated.
32 devices in a mesh: seg: 4 (over y, x), bin: 8 (over z, core).
Axes of the slice: x: 2, y: 2, z: 4, core: 2. Of those that a mesh axis runs over, the one named last changes fastest.
Arguments:
- coverage_lanes: bfloat16 [256, 128, 128], P(('seg', 'bin')), may hold values from 4 to 64
- target_blocks: int32 [256], P(('seg', 'bin')), may hold values from 0 to 7, as said below
- valid_bins: int32 [256], P(('seg', 'bin')), may hold values from 1 to 128
- panel_mean: float32 [32768], P(('seg', 'bin')), may hold values from 3.5 to 5
- components: float32 [256, 32768], P(None, ('seg', 'bin')), as said below
- kernels: float32 [3, 33, 32768], P(None, None, ('seg', 'bin')), may hold values from 0 to 0.08
- chrom_starts: int32 [24], replicated, may hold values from 0 to 32767, as said below
Outputs:
- coefficients: float32 [128, 256], replicated
- smoothed: float32 [128, 32768], P(None, ('seg', 'bin'))
- bridge: float32 [128, 32768], P(None, ('seg', 'bin'))
Inputs may be any that keep to these rules, and one draw needn't show every extreme that they name: target_blocks names one of the owner's 8 blocks; slot r of a device goes to the owner given by r // 1 within the device's stretch. `chrom_starts`: strictly rising chromosome starts, the first is 0 and the last is 32767. panel-of-normals components.
All inputs are finite; a program needn't handle non-finite values.
Results may differ from a plain program's by a relative error of at most 0.0003.
Values may be sent and summed in bfloat16 or wider, within the bound.
A program may use at most 192 MiB of HBM per device.

v0:
```python
import math

import jax
import jax.numpy as jnp
from jax import lax
from jax.sharding import PartitionSpec as P


def extended(block, sides, width):
    for axis, dim in sides:
        count = lax.axis_size(axis)
        forward = [(i, i + 1) for i in range(count - 1)]
        backward = [(target, source) for source, target in forward]
        low = lax.ppermute(
            lax.slice_in_dim(block, block.shape[dim] - width, None, axis=dim), axis, forward
        )
        high = lax.ppermute(lax.slice_in_dim(block, 0, width, axis=dim), axis, backward)
        block = jnp.concatenate([low, block, high], axis=dim)
    return block


def prefix(part, axis, combine, identity):
    place = lax.axis_index(axis)
    gathered = lax.all_gather(part, axis)
    state = jnp.zeros_like(part) + jnp.asarray(identity, part.dtype)

    def one(hop, state):
        return combine(state, lax.dynamic_index_in_dim(gathered, hop, 0, False))

    return lax.fori_loop(0, place, one, state)


def chrom_labels(chrom_starts, first_bin, count, total_bins):
    positions = first_bin + lax.iota(jnp.int32, count)
    covered = jnp.sum((chrom_starts[:, None] <= positions[None, :]).astype(jnp.int32), axis=0) - 1
    return jnp.where(positions >= total_bins, chrom_starts.shape[0], covered)


def smooth_once(padded, tap_weights, labels, out_width):
    half_taps = (tap_weights.shape[0] - 1) // 2
    centre = labels[half_taps : half_taps + out_width]
    result = jnp.zeros((padded.shape[0], out_width), jnp.float32)
    for tap_index in range(tap_weights.shape[0]):
        weight = tap_weights[tap_index] * (
            labels[tap_index : tap_index + out_width] == centre
        ).astype(jnp.float32)
        result = result + weight[None, :] * padded[:, tap_index : tap_index + out_width]
    return result


def add_terms(earlier, later):
    return earlier + later


def per_device(
    coverage_lanes, target_blocks, valid_bins, panel_mean, components, kernels, chrom_starts
):
    slot_count, samples, block_bins = coverage_lanes.shape
    bin_dev = panel_mean.shape[0]
    blocks_dev = bin_dev // block_bins
    total_bins = bin_dev * lax.axis_size(("seg", "bin"))
    first_bin = lax.axis_index(("seg", "bin")) * bin_dev
    keep_mask = (lax.iota(jnp.int32, block_bins)[None, :] < valid_bins[:, None]).astype(
        jnp.bfloat16
    )
    masked = coverage_lanes * keep_mask[:, None, :]
    arrived, arrived_targets = (
        lax.all_to_all(masked, "bin", split_axis=0, concat_axis=0, tiled=True),
        lax.all_to_all(
            target_blocks.astype(jnp.bfloat16), "bin", split_axis=0, concat_axis=0, tiled=True
        ),
    )
    block_names = lax.iota(jnp.int32, blocks_dev).astype(jnp.bfloat16)
    placing = (arrived_targets[None, :] == block_names[:, None]).astype(jnp.bfloat16)
    coverage = jnp.einsum("br,rsc->sbc", placing, arrived, preferred_element_type=jnp.float32)
    coverage = coverage.reshape(samples, bin_dev)
    log_ratio = jnp.log(coverage + 1.0) - panel_mean[None, :]
    partial_terms = lax.dot_general(
        log_ratio,
        components,
        (((1,), (1,)), ((), ())),
        precision=lax.Precision.HIGHEST,
        preferred_element_type=jnp.float32,
    )
    coefficients = lax.psum(partial_terms, ("seg", "bin"))
    signal = log_ratio - jnp.dot(
        coefficients,
        components,
        precision=lax.Precision.HIGHEST,
        preferred_element_type=jnp.float32,
    )
    layers = kernels.shape[0]
    half_taps = (kernels.shape[1] - 1) // 2
    labels = chrom_labels(chrom_starts, first_bin - half_taps, bin_dev + 2 * half_taps, total_bins)
    smoothed = signal
    for layer_index in range(layers):
        padded = extended(smoothed, ((("seg", "bin"), 1),), half_taps)
        smoothed = smooth_once(padded, kernels[layer_index], labels, bin_dev)
    totals = lax.psum(jnp.sum(smoothed, axis=1), ("seg", "bin"))
    centred = smoothed - (totals / total_bins)[:, None]
    blocks_view = centred.reshape(samples, blocks_dev, block_bins)
    upper_ones = (
        lax.iota(jnp.int32, block_bins)[:, None] <= lax.iota(jnp.int32, block_bins)[None, :]
    ).astype(jnp.float32)
    inside = jnp.einsum(
        "snc,cd->snd",
        blocks_view,
        upper_ones,
        precision=lax.Precision.HIGHEST,
        preferred_element_type=jnp.float32,
    )
    block_sums = inside[:, :, -1]
    running = jnp.cumsum(block_sums, axis=1)
    local_prefix = inside + (running - block_sums)[:, :, None]
    local_total = running[:, -1]
    zero_terms = jnp.zeros_like(local_total)
    before = prefix(local_total, ("seg", "bin"), add_terms, zero_terms)
    bridge = (local_prefix.reshape(samples, bin_dev) + before[:, None]) * (
        1.0 / math.sqrt(total_bins)
    )
    return (coefficients, smoothed, bridge)


def solution(mesh):
    in_specs = (
        P(("seg", "bin"), None, None),
        P(("seg", "bin")),
        P(("seg", "bin")),
        P(("seg", "bin")),
        P(None, ("seg", "bin")),
        P(None, None, ("seg", "bin")),
        P(),
    )
    out_specs = (P(), P(None, ("seg", "bin")), P(None, ("seg", "bin")))
    return jax.shard_map(
        per_device, mesh=mesh, in_specs=in_specs, out_specs=out_specs, check_vma=False
    )
```

profile of v0, /device:TPU:0, one launch (start us, length us, event | category | flops | bytes accessed | tf_op | source)
XLA Modules:
  0.0 307.0 jit_solution(12977762061642653183)
XLA Ops:
  7.2 0.7 convert_bitcast_fusion
  7.9 0.7 copy.21
  8.6 6.3 %all-to-all-start.1 = ((bf16[8,1,1]{2,1,0:T(2,128)(2,1)}), bf16[8,1,1]{2,1,0:T(2,128)(2,1)S(1)}, u32[]{:S(2)}, u32[]{:S(2)}) async-start(bf16[8,1,1]{2,1,0:T(2,128)(2,1)} %copy.21), calls=%async_computation.1 | async-start | bytes 8192 | tf_op jit(solution)/shard_map/all_to_all | solution.py:69
  14.9 0.8 fusion.306
  15.8 1.4 fusion.303
  17.1 1.4 fusion.305
  18.5 1.4 fusion.302
  19.9 1.4 fusion.301
  21.3 1.7 fusion.304
  23.7 0.6 copy-done.6
  24.4 0.7 broadcast_multiply_fusion
  25.8 5.1 %all-to-all-start = ((bf16[8,128,128]{2,1,0:T(8,128)(2,1)}), bf16[8,128,128]{2,1,0:T(8,128)(2,1)S(1)}, u32[]{:S(2)}, u32[]{:S(2)}) async-start(bf16[8,128,128]{2,1,0:T(8,128)(2,1)} %broadcast_multiply_fusion), calls=%async_computation | async-start | bytes 524288 | tf_op jit(solution)/shard_map/all_to_all | solution.py:68
  31.2 9.5 %all-to-all-done = bf16[8,128,128]{2,1,0:T(8,128)(2,1)S(1)} async-done(((bf16[8,128,128]{2,1,0:T(8,128)(2,1)}), bf16[8,128,128]{2,1,0:T(8,128)(2,1)S(1)}, u32[]{:S(2)}, u32[]{:S(2)}) %all-to-all-start) | async-done | bytes 262176 | tf_op jit(solution)/shard_map/all_to_all | solution.py:68
  41.4 1.9 fusion.286
  43.3 121.5 %all-reduce.2.cloned.1.call-done = f32[128,256]{1,0:T(8,128)} async-done(((f32[128,256]{1,0:T(8,128)}), f32[128,256]{1,0:T(8,128)}) %all-reduce.2.cloned.1.call-update) | async-done | bytes 131088 | tf_op jit(solution)/shard_map/psum | solution.py:85
  164.7 1.7 convolution_subtract_fusion
  166.5 1.3 collective-permute-start
  167.8 1.3 collective-permute-start.1
  169.1 3.5 %collective-permute-done.1 = f32[128,16]{1,0:T(8,128)S(1)} collective-permute-done((f32[128,16]{1,0:T(8,128)S(1)}, f32[128,16]{1,0:T(8,128)S(1)}, u32[]{:S(2)}, u32[]{:S(2)}) %collective-permute-start.1) | collective-permute-done | bytes 8224 | tf_op jit(solution)/shard_map/ppermute | solution.py:17
  172.6 6.0 %fusion.188 = f32[128,1024]{1,0:T(8,128)S(1)} fusion(f32[128,1024]{1,0:T(8,128)S(1)} %convolution_subtract_fusion, f32[128,16]{1,0:T(8,128)S(1)} %collective-permute-done.1, f32[128,16]{1,0:T(8,128)S(1)} %collective-permute-done, f32[1024]{0:T(1024)S(1)} %get-tuple-element.321, f32[1024]{0:T(1024)S(1)} %get-tuple-element.319, ...), kind=kLoop, calls=%fused_computation.371 | loop fusion | flops 12713984 | bytes 1200128 | tf_op jit(solution)/shard_map/add | solution.py:47
  178.7 4.8 %collective-permute-start.2 = (f32[128,16]{1,0:T(8,128)S(1)}, f32[128,16]{1,0:T(8,128)S(1)}, u32[]{:S(2)}, u32[]{:S(2)}) collective-permute-start(f32[128,16]{1,0:T(8,128)S(1)} %get-tuple-element.103), channel_id=1, source_target_pairs={{0,1},{1,2},{2,3},{3,4},{4,5},{5,6},{6,7},{7,8},{8,9},{9,10},{10,1... | collective-permute-start | bytes 24584 | tf_op jit(solution)/shard_map/ppermute | solution.py:14
  183.5 1.3 collective-permute-start.3
  184.8 1.8 collective-permute-done.3
  186.7 6.0 %fusion.96 = f32[128,1024]{1,0:T(8,128)S(1)} fusion(f32[128,1024]{1,0:T(8,128)S(1)} %fusion.188, f32[128,16]{1,0:T(8,128)S(1)} %collective-permute-done.3, f32[128,16]{1,0:T(8,128)S(1)} %collective-permute-done.2, f32[1024]{0:T(1024)S(1)} %get-tuple-element.320, f32[1024]{0:T(1024)S(1)} %get-tuple-element.318, f32[1024]{0:T(1024)S(1)} %get-tuple-element.325, ...), kind=kLoop, calls=%fused_computation.279 | loop fusion | flops 12713984 | bytes 1200128 | tf_op jit(solution)/shard_map/add | solution.py:47
  192.7 4.4 %collective-permute-start.4 = (f32[128,16]{1,0:T(8,128)S(1)}, f32[128,16]{1,0:T(8,128)S(1)}, u32[]{:S(2)}, u32[]{:S(2)}) collective-permute-start(f32[128,16]{1,0:T(8,128)S(1)} %get-tuple-element.101), channel_id=1, source_target_pairs={{0,1},{1,2},{2,3},{3,4},{4,5},{5,6},{6,7},{7,8},{8,9},{9,10},{10,1... | collective-permute-start | bytes 24584 | tf_op jit(solution)/shard_map/ppermute | solution.py:14
  197.1 1.5 collective-permute-start.5
  198.6 1.7 collective-permute-done.5
  200.3 7.3 %fusion.296 = (f32[128]{0:T(128)S(1)}, f32[128,1024]{1,0:T(8,128)S(1)}) fusion(f32[128,16]{1,0:T(8,128)S(1)} %collective-permute-done.5, f32[128,1024]{1,0:T(8,128)S(1)} %fusion.96, f32[1024]{0:T(1024)S(1)} %get-tuple-element.256, f32[1024]{0:T(1024)S(1)} %get-tuple-element.206, f32[1024]{0:T(1024)S(1)} %get-tuple-element.208, ...), kind=kLoop, calls=%fused_computation.626 | loop fusion | flops 12844928 | bytes 1200640 | tf_op jit(solution)/shard_map/reduce_sum | solution.py:99
  207.6 51.3 %psum.15 = f32[128]{0:T(128)S(1)} all-reduce(f32[128]{0:T(128)S(1)} %get-tuple-element.35), channel_id=1, replica_groups=mesh['seg'=4,'bin'=8] {'seg','bin'}, use_global_device_ids=true, to_apply=%region_3.4 | all-reduce | flops 128 | bytes 1024 | tf_op jit(solution)/shard_map/psum | solution.py:99
  259.7 38.8 %all-gather = f32[4096,1]{0,1:T(1,128)S(1)} all-gather(f32[128,1]{0,1:T(1,128)S(1)} %slice.1309), channel_id=2, replica_groups=mesh['seg'=4,'bin'=8] {'seg','bin'}, dimensions={0}, use_global_device_ids=true | all-gather | bytes 16896 | tf_op jit(solution)/shard_map/all_gather | solution.py:24
  298.5 0.9 add_multiply_fusion
  299.5 0.7 copy.44
  (61 shorter events, 3.4 us)
Async XLA Ops:
  7.2 33.8 %copy-start = (f32[256,1024]{1,0:T(8,128)S(1)}, f32[256,1024]{1,0:T(8,128)}, u32[]{:S(2)}) copy-start(f32[256,1024]{1,0:T(8,128)} %param.13) | copy-start | bytes 3145732
  8.6 17.2 %all-to-all-start.1 = ((bf16[8,1,1]{2,1,0:T(2,128)(2,1)}), bf16[8,1,1]{2,1,0:T(2,128)(2,1)S(1)}, u32[]{:S(2)}, u32[]{:S(2)}) async-start(bf16[8,1,1]{2,1,0:T(2,128)(2,1)} %copy.21), calls=%async_computation.1 | async-start | bytes 8192 | tf_op jit(solution)/shard_map/all_to_all | solution.py:69
  18.5 5.9 %copy-start.3 = (bf16[8,128,128]{2,1,0:T(8,128)(2,1)S(1)}, bf16[8,128,128]{2,1,0:T(8,128)(2,1)}, u32[]{:S(2)}) copy-start(bf16[8,128,128]{2,1,0:T(8,128)(2,1)} %param.9) | copy-start | bytes 786436
  22.9 0.7 copy-start.5
  23.7 0.7 copy-start.6
  25.8 14.9 %all-to-all-start = ((bf16[8,128,128]{2,1,0:T(8,128)(2,1)}), bf16[8,128,128]{2,1,0:T(8,128)(2,1)S(1)}, u32[]{:S(2)}, u32[]{:S(2)}) async-start(bf16[8,128,128]{2,1,0:T(8,128)(2,1)} %broadcast_multiply_fusion), calls=%async_computation | async-start | bytes 524288 | tf_op jit(solution)/shard_map/all_to_all | solution.py:68
  31.0 133.8 %all-reduce.2.cloned.1.call-start = ((), (), s32[]{:S(2)}) async-start(), calls=%async_computation.2 | async-start | bytes 262144 | tf_op jit(solution)/shard_map/psum | solution.py:85
  40.7 0.7 copy-start.4
  166.5 2.6 collective-permute-start
  167.8 4.8 %collective-permute-start.1 = (f32[128,16]{1,0:T(8,128)S(1)}, f32[128,16]{1,0:T(8,128)S(1)}, u32[]{:S(2)}, u32[]{:S(2)}) collective-permute-start(f32[128,16]{1,0:T(8,128)S(1)} %get-tuple-element.106), channel_id=1, source_target_pairs={{1,0},{2,1},{3,2},{4,3},{5,4},{6,5},{7,6},{8,7},{9,8},{10,9},{11,1... | collective-permute-start | bytes 24584 | tf_op jit(solution)/shard_map/ppermute | solution.py:17
  178.7 6.1 %collective-permute-start.2 = (f32[128,16]{1,0:T(8,128)S(1)}, f32[128,16]{1,0:T(8,128)S(1)}, u32[]{:S(2)}, u32[]{:S(2)}) collective-permute-start(f32[128,16]{1,0:T(8,128)S(1)} %get-tuple-element.103), channel_id=1, source_target_pairs={{0,1},{1,2},{2,3},{3,4},{4,5},{5,6},{6,7},{7,8},{8,9},{9,10},{10,1... | collective-permute-start | bytes 24584 | tf_op jit(solution)/shard_map/ppermute | solution.py:14
  183.5 3.1 %collective-permute-start.3 = (f32[128,16]{1,0:T(8,128)S(1)}, f32[128,16]{1,0:T(8,128)S(1)}, u32[]{:S(2)}, u32[]{:S(2)}) collective-permute-start(f32[128,16]{1,0:T(8,128)S(1)} %get-tuple-element.104), channel_id=1, source_target_pairs={{1,0},{2,1},{3,2},{4,3},{5,4},{6,5},{7,6},{8,7},{9,8},{10,9},{11,1... | collective-permute-start | bytes 24584 | tf_op jit(solution)/shard_map/ppermute | solution.py:17
  192.7 5.8 %collective-permute-start.4 = (f32[128,16]{1,0:T(8,128)S(1)}, f32[128,16]{1,0:T(8,128)S(1)}, u32[]{:S(2)}, u32[]{:S(2)}) collective-permute-start(f32[128,16]{1,0:T(8,128)S(1)} %get-tuple-element.101), channel_id=1, source_target_pairs={{0,1},{1,2},{2,3},{3,4},{4,5},{5,6},{6,7},{7,8},{8,9},{9,10},{10,1... | collective-permute-start | bytes 24584 | tf_op jit(solution)/shard_map/ppermute | solution.py:14
  197.1 3.1 %collective-permute-start.5 = (f32[128,16]{1,0:T(8,128)S(1)}, f32[128,16]{1,0:T(8,128)S(1)}, u32[]{:S(2)}, u32[]{:S(2)}) collective-permute-start(f32[128,16]{1,0:T(8,128)S(1)} %get-tuple-element.102), channel_id=1, source_target_pairs={{1,0},{2,1},{3,2},{4,3},{5,4},{6,5},{7,6},{8,7},{9,8},{10,9},{11,1... | collective-permute-start | bytes 24584 | tf_op jit(solution)/shard_map/ppermute | solution.py:17
  207.6 51.8 %copy-start.1 = (f32[128,1024]{1,0:T(8,128)}, f32[128,1024]{1,0:T(8,128)S(1)}, u32[]{:S(2)}) copy-start(f32[128,1024]{1,0:T(8,128)S(1)} %get-tuple-element.402) | copy-start | bytes 1572868
  298.5 0.9 copy-start.2
Sparse Core Ops, SparseCore 0:
  43.4 121.3 all-reduce.1
where the time goes:
time: 308 us; the launch traced here: 307 us
  waiting for transfers between devices  138 us (45%)
  blocking collectives  90.1 us (29%)
  starting transfers between devices  26 us (8%)
  other arithmetic  22.6 us (7%)
  between operations  14.4 us (5%)
  local copies, waits for them, and re-layouts  11.5 us (4%)
  matrix products  4.31 us (1%)
    psum x1, waiting for transfers between devices, per_device(): coefficients = lax.psum(partial_terms, ('seg', 'bin'))  121 us
    psum x1, blocking collectives, per_device(): totals = lax.psum(jnp.sum(smoothed, axis=1), ('seg', 'bin'))  51.3 us
    all_gather x1, blocking collectives, prefix(): gathered = lax.all_gather(part, axis)  38.8 us
    add x2, other arithmetic, smooth_once(): result + weight[None, :] * padded[:, tap_index:tap_index + out_width]  12 us
    ppermute x3, starting transfers between devices, extended(): lax.ppermute(lax.slice_in_dim(block, block.shape[dim] - width, None, axis...  10.5 us
    all_to_all x1, waiting for transfers between devices, per_device(): lax.all_to_all(masked, 'bin', split_axis=0, concat_axis=0, tiled=True)  9.51 us
    slice x6, local copies, waits for them, and re-layouts, smooth_once(): tap_weights[tap_index]  7.96 us
    reduce_sum x1, other arithmetic, per_device(): totals = lax.psum(jnp.sum(smoothed, axis=1), ('seg', 'bin'))  7.3 us
  transfers between devices with their start and end apart: 9, of which 5 were waited for; matrix products, arithmetic and copies ran while one was open for 3% of the time, Pallas kernels for 0%

commit v1 on v0

v1 whole, which is shorter than its diff:
```python
import functools
import math

import jax
import jax.numpy as jnp
from jax import lax
from jax.experimental import pallas as pl
from jax.experimental.pallas import tpu as pltpu
from jax.sharding import PartitionSpec as P

MESH = pl.DeviceIdType.MESH
F32, BF16 = jnp.float32, jnp.bfloat16
LANES = 128


def split(x):
    high = x.astype(BF16)
    return high, (x - high.astype(F32)).astype(BF16)


def mm(a, b, contract=(1, 0)):
    return lax.dot_general(
        a, b, (((contract[0],), (contract[1],)), ((), ())), preferred_element_type=F32
    )


def iota(shape, dim):
    return lax.broadcasted_iota(jnp.int32, shape, dim)


def wait_bytes(ref, sem):
    pltpu.make_async_copy(ref, ref, sem).wait()


def body(
    nseg, nb, targets, valid, starts, lanes, panel, comp, kern,
    coef_o, smooth_o, bridge_o,
    send_l, recv_l, kx, taps, lrx, kh, kl, lh, ll, ah, al, bh, bl,
    skh, skl, weights, part, gathered, c2, sums, ssem, rsem, lsem,
):
    ndev = nseg * nb
    seg, place = lax.axis_index("seg"), lax.axis_index("bin")
    me = seg * nb + place
    samples, bin_dev = smooth_o.shape
    comps = kx.shape[0]
    blocks = bin_dev // LANES
    total_bins = bin_dev * ndev
    first = me * bin_dev
    ntaps = kern.shape[1]
    half = (ntaps - 1) // 2

    def dev(flat):
        return (lax.div(flat, nb), lax.rem(flat, nb))

    def remote(src, dst, which, device):
        return pltpu.make_async_remote_copy(
            src_ref=src, dst_ref=dst, send_sem=ssem.at[which], recv_sem=rsem.at[which],
            device_id=device, device_id_type=MESH,
        )

    barrier = pltpu.get_barrier_semaphore()

    @pl.loop(1, ndev)
    def _(hop):
        pl.semaphore_signal(
            barrier, inc=1, device_id=dev(lax.rem(me + hop, ndev)), device_id_type=MESH
        )

    own_k = pltpu.make_async_copy(comp, kx.at[:, pl.ds(LANES, bin_dev)], lsem.at[0])
    own_k.start()
    own_t = pltpu.make_async_copy(kern, taps.at[:, :, pl.ds(LANES, bin_dev)], lsem.at[1])
    own_t.start()

    @pl.loop(0, nb)
    def _(r):
        keep = iota((samples, LANES), 1) < valid[r]
        send_l[r, :samples, :] = jnp.where(keep, lanes[r].astype(F32), 0.0).astype(BF16)
        mark = jnp.full((16, LANES), targets[r], jnp.int32).astype(F32)
        send_l[r, samples:, :] = mark.astype(BF16)

    pl.semaphore_wait(barrier, ndev - 1)

    @pl.loop(1, nb)
    def _(hop):
        to = lax.rem(place + hop, nb)
        remote(send_l.at[to], recv_l.at[place], 0, (seg, to)).start()

    right, left = dev(lax.rem(me + 1, ndev)), dev(lax.rem(me + ndev - 1, ndev))
    low, high = pl.ds(0, LANES), pl.ds(bin_dev + LANES, LANES)
    head, tail = pl.ds(0, LANES), pl.ds(bin_dev - LANES, LANES)
    halos = [
        remote(kern.at[pl.ds(0, 2), :, tail], taps.at[pl.ds(0, 2), :, low], 1, right),
        remote(kern.at[pl.ds(0, 2), :, head], taps.at[pl.ds(0, 2), :, high], 2, left),
        remote(comp.at[:, tail], kx.at[:, low], 3, right),
        remote(comp.at[:, head], kx.at[:, high], 4, left),
    ]
    for copy in halos:
        copy.start()

    recv_l[place] = send_l[place]

    own_t.wait()
    halos[0].wait_recv()
    halos[1].wait_recv()

    def band(layer, m, offset, top):
        if offset == LANES:
            columns = pl.ds(pl.multiple_of((m + 1) * LANES, LANES), LANES)
            upper = taps[layer, : 2 * half, columns]
            last = taps[layer, 2 * half : ntaps, columns]
        else:
            columns = pl.ds(pl.multiple_of(m * LANES, LANES), 2 * LANES)
            upper = taps[layer, : 2 * half, columns]
            last = taps[layer, 2 * half : ntaps, columns]
        last = jnp.broadcast_to(last, (8, last.shape[1]))
        last = jnp.where(iota(last.shape, 0) == 0, last, 0.0)
        rows = jnp.concatenate([upper, last], axis=0)
        if offset != LANES:
            rows = pltpu.roll(rows, 2 * LANES - offset, 1)[:, :LANES]
        position = first - LANES + offset + m * LANES + iota((8, LANES), 1)
        lower = jnp.full((8, LANES), total_bins, jnp.int32)
        upto = jnp.where(position < total_bins, total_bins, -1)
        count = starts.shape[0]
        for k in range(count):
            lower = jnp.where(starts[k] <= position, starts[k], lower)
        for k in range(count - 1, -1, -1):
            upto = jnp.where(starts[k] > position, starts[k], upto)
        tall = rows.shape[0]
        source = position[:1] + iota((tall, LANES), 0) - half
        inside = (source >= lower[:1]) & (source < upto[:1])
        rows = jnp.where(inside, rows, 0.0)
        lane = iota((1, LANES), 1)
        step = 1
        while step < LANES:
            if step < 8:
                moved = pltpu.roll(rows, step, 0)
                still = rows
            else:
                pad = jnp.zeros((step, LANES), F32)
                moved = jnp.concatenate([pad, rows], axis=0)
                still = jnp.concatenate([rows, pad], axis=0)
            chosen = jnp.broadcast_to((lane & step) != 0, moved.shape)
            rows = jnp.where(chosen, moved, still)
            step *= 2
        rest = 2 * LANES - rows.shape[0] - top
        pieces = [rows, jnp.zeros((rest, LANES), F32)]
        if top:
            pieces = [jnp.zeros((top, LANES), F32)] + pieces
        return split(jnp.concatenate(pieces, axis=0))

    plan = (
        (0, LANES - 2 * half, LANES - 3 * half, 0, blocks + 1),
        (1, LANES - half, 0, blocks + 1, blocks + 1),
        (2, LANES, 0, 2 * blocks + 2, blocks),
    )
    for layer, offset, top, base, many in plan:

        @pl.loop(0, many)
        def _(m, layer=layer, offset=offset, top=top, base=base):
            w_high, w_low = band(layer, m, offset, top)
            weights[base + m, :, :LANES] = w_high
            weights[base + m, :, LANES:] = w_low

    def smooth_pass(src_high, src_low, m, base):
        window = pl.ds(m * LANES, 2 * LANES)
        both = mm(src_high[:, window], weights[base + m])
        return both[:, :LANES] + both[:, LANES:] + mm(
            src_low[:, window], weights[base + m, :, :LANES]
        )

    def smooth(src, mid, end, rows, store):
        for m in range(blocks + 1):
            out = split(smooth_pass(src[0], src[1], m, plan[0][3]))
            for ref, value in zip(mid, out):
                ref[:rows, pl.ds(m * LANES, LANES)] = value
        for m in range(blocks + 1):
            out = split(
                smooth_pass(mid[0].at[:rows], mid[1].at[:rows], m, plan[1][3])
            )
            for ref, value in zip(end, out):
                ref[:rows, pl.ds(m * LANES, LANES)] = value
        total = jnp.zeros((rows, LANES), F32)
        for m in range(blocks):
            out = smooth_pass(end[0].at[:rows], end[1].at[:rows], m, plan[2][3])
            store(m, out)
            total = total + out
        return jnp.sum(total, axis=1, keepdims=True)

    eye = iota((LANES, LANES), 0) == iota((LANES, LANES), 1)

    def as_row(column):
        return jnp.sum(jnp.where(eye, column, 0.0), axis=0, keepdims=True)

    own_k.wait()
    halos[2].wait_recv()
    halos[3].wait_recv()
    for ref in (ah, al, bh, bl):
        ref[:, pl.ds(bin_dev + LANES, LANES)] = jnp.zeros((comps, LANES), BF16)
    kh[...], kl[...] = split(kx[...])

    def store_k(m, out):
        window = pl.ds(m * LANES, LANES)
        skh[:, window], skl[:, window] = split(out)

    k_total = smooth((kh, kl), (ah, al), (bh, bl), comps, store_k)

    wait_bytes(recv_l.at[pl.ds(0, nb - 1)], rsem.at[0])
    for b in range(blocks):

        def add(r, acc):
            mark = recv_l[r, samples : samples + 16, :].astype(F32)[:1]
            return acc + jnp.where(
                jnp.broadcast_to(mark == float(b), acc.shape),
                recv_l[r, :samples, :].astype(F32), 0.0,
            )

        cover = lax.fori_loop(0, nb, add, jnp.zeros((samples, LANES), F32), unroll=nb <= 8)
        window = pl.ds(b * LANES, LANES)
        lrx[:, pl.ds((b + 1) * LANES, LANES)] = jnp.log(cover + 1.0) - panel[:, window]

    near = [
        remote(lrx.at[:, pl.ds(bin_dev, LANES)], lrx.at[:, low], 5, right),
        remote(lrx.at[:, pl.ds(LANES, LANES)], lrx.at[:, high], 6, left),
    ]
    for copy in near:
        copy.start()

    own = pl.ds(LANES, bin_dev)
    lh[:, own], ll[:, own] = split(lrx[:, own])
    terms = (
        mm(lh[:, own], kh[:, own], (1, 1))
        + mm(ll[:, own], kh[:, own], (1, 1))
        + mm(lh[:, own], kl[:, own], (1, 1))
    )
    for h in range(comps // LANES):
        part[pl.ds(h * samples, samples), :] = terms[:, h * LANES : (h + 1) * LANES]

    tiles = part.shape[0] // 8
    stride = ndev // tiles
    mine = lax.div(me, stride)
    owner = lax.rem(me, stride) == 0

    def tile(j):
        return pl.ds(pl.multiple_of(j * 8, 8), 8)

    @pl.loop(1 if stride == 1 else 0, tiles)
    def _(hop):
        j = lax.rem(mine + hop, tiles)
        copy = remote(part.at[tile(j)], gathered.at[me], 7, dev(j * stride))
        if stride == 1:
            copy.start()
        else:
            pl.when(j * stride != me)(copy.start)

    for copy in near:
        copy.wait_recv()
    for edge in (low, high):
        lh[:, edge], ll[:, edge] = split(lrx[:, edge])

    def store_l(m, out):
        smooth_o[:, pl.ds(m * LANES, LANES)] = out

    l_total = smooth((lh, ll), (ah, al), (bh, bl), samples, store_l)
    sums[me] = jnp.concatenate(
        [as_row(l_total)]
        + [as_row(k_total[h * LANES : (h + 1) * LANES]) for h in range(comps // LANES)]
        + [jnp.zeros((7 - comps // LANES, LANES), F32)],
        axis=0,
    )

    def reduce_and_send():
        gathered[me] = part[tile(mine), :]
        wait_bytes(gathered.at[pl.ds(0, ndev - 1)], rsem.at[7])
        c2[tile(mine), :] = jnp.sum(gathered[...], axis=0)

        @pl.loop(1, ndev)
        def _(hop):
            to = dev(lax.rem(me + hop, ndev))
            remote(c2.at[tile(mine)], c2.at[tile(mine)], 8, to).start()

    if stride == 1:
        reduce_and_send()
    else:
        pl.when(owner)(reduce_and_send)

    @pl.loop(1, ndev)
    def _(hop):
        remote(sums.at[me], sums.at[me], 9, dev(lax.rem(me + hop, ndev))).start()

    if stride == 1:
        wait_bytes(c2.at[pl.ds(0, 8 * (tiles - 1))], rsem.at[8])
    else:

        @pl.when(owner)
        def _():
            wait_bytes(c2.at[pl.ds(0, 8 * (tiles - 1))], rsem.at[8])

        @pl.when(jnp.logical_not(owner))
        def _():
            wait_bytes(c2, rsem.at[8])

    coef = jnp.concatenate(
        [c2[pl.ds(h * samples, samples), :] for h in range(comps // LANES)], axis=1
    )
    coef_o[...] = coef
    c_high, c_low = split(coef)
    smooth_o[...] = smooth_o[...] - (
        mm(c_high, skh[...]) + mm(c_low, skh[...]) + mm(c_high, skl[...])
    )

    wait_bytes(sums.at[pl.ds(0, ndev - 1)], rsem.at[9])
    every = jnp.sum(sums[...], axis=0)
    part_mean = every * (1.0 / ndev)

    def earlier(q, acc):
        return acc + jnp.where(q < me, 1.0, 0.0) * (sums[q] - part_mean)

    before_rows = lax.fori_loop(0, ndev, earlier, jnp.zeros((8, LANES), F32), unroll=ndev <= 32)

    def resolve(rows):
        level = jnp.where(eye, jnp.broadcast_to(rows[:1], (LANES, LANES)), 0.0)
        for h in range(comps // LANES):
            level = level - coef[:, h * LANES : (h + 1) * LANES] * rows[h + 1 : h + 2]
        return jnp.sum(level, axis=1, keepdims=True)

    mean = resolve(part_mean) * (1.0 / bin_dev)
    carry = resolve(before_rows)
    wide = 2 * LANES
    ones = jnp.where(iota((wide, wide), 0) <= iota((wide, wide), 1), 1.0, 0.0).astype(BF16)
    scale = 1.0 / math.sqrt(total_bins)
    for m in range(bin_dev // wide):
        window = pl.ds(m * wide, wide)
        v_high, v_low = split(smooth_o[:, window] - mean)
        run = mm(v_high, ones) + mm(v_low, ones) + carry
        bridge_o[:, window] = run * scale
        carry = run[:, wide - 1 :]

    wait_bytes(send_l.at[pl.ds(0, nb - 1)], ssem.at[0])
    for copy in halos + near:
        copy.wait_send()
    wait_bytes(sums.at[pl.ds(0, ndev - 1)], ssem.at[9])
    if stride == 1:
        wait_bytes(part.at[pl.ds(0, 8 * (tiles - 1))], ssem.at[7])
        wait_bytes(gathered.at[pl.ds(0, ndev - 1)], ssem.at[8])
    else:

        @pl.when(owner)
        def _():
            wait_bytes(part.at[pl.ds(0, 8 * (tiles - 1))], ssem.at[7])
            wait_bytes(gathered.at[pl.ds(0, ndev - 1)], ssem.at[8])

        @pl.when(jnp.logical_not(owner))
        def _():
            wait_bytes(part, ssem.at[7])


def solution(mesh):
    nseg, nb = mesh.shape["seg"], mesh.shape["bin"]
    ndev = nseg * nb

    def per_device(lanes, targets, valid, panel, comp, kern, starts):
        samples = lanes.shape[1]
        comps, bin_dev = comp.shape
        layers, ntaps = kern.shape[:2]
        ext = bin_dev + 2 * LANES
        bands = 3 * (bin_dev // LANES) + 2
        vmem, smem = pltpu.VMEM, pltpu.SMEM
        whole = pl.BlockSpec(memory_space=vmem)
        scalar = pl.BlockSpec(memory_space=smem)
        away = pl.BlockSpec(memory_space=pl.ANY)
        return pl.pallas_call(
            functools.partial(body, nseg, nb),
            out_shape=(
                jax.ShapeDtypeStruct((samples, comps), F32),
                jax.ShapeDtypeStruct((samples, bin_dev), F32),
                jax.ShapeDtypeStruct((samples, bin_dev), F32),
            ),
            in_specs=[scalar, scalar, scalar, whole, whole, away, away],
            out_specs=(whole, whole, whole),
            scratch_shapes=[
                vmem((nb, samples + 16, LANES), BF16),
                vmem((nb, samples + 16, LANES), BF16),
                vmem((comps, ext), F32),
                vmem((layers, ntaps, ext), F32),
                vmem((samples, ext), F32),
                vmem((comps, ext), BF16),
                vmem((comps, ext), BF16),
                vmem((samples, ext), BF16),
                vmem((samples, ext), BF16),
                vmem((comps, ext), BF16),
                vmem((comps, ext), BF16),
                vmem((comps, ext), BF16),
                vmem((comps, ext), BF16),
                vmem((comps, bin_dev), BF16),
                vmem((comps, bin_dev), BF16),
                vmem((bands, 2 * LANES, 2 * LANES), BF16),
                vmem((samples * comps // LANES, LANES), F32),
                vmem((ndev, 8, LANES), F32),
                vmem((samples * comps // LANES, LANES), F32),
                vmem((ndev, 8, LANES), F32),
                pltpu.SemaphoreType.DMA((10,)),
                pltpu.SemaphoreType.DMA((10,)),
                pltpu.SemaphoreType.DMA((2,)),
            ],
            compiler_params=pltpu.CompilerParams(
                collective_id=0, has_side_effects=True, vmem_limit_bytes=48 << 20
            ),
        )(targets, valid, starts, lanes, panel.reshape(1, bin_dev), comp, kern)

    in_specs = (
        P(("seg", "bin"), None, None),
        P(("seg", "bin")),
        P(("seg", "bin")),
        P(("seg", "bin")),
        P(None, ("seg", "bin")),
        P(None, None, ("seg", "bin")),
        P(),
    )
    out_specs = (P(), P(None, ("seg", "bin")), P(None, ("seg", "bin")))
    return jax.shard_map(
        per_device, mesh=mesh, in_specs=in_specs, out_specs=out_specs, check_vma=False
    )
```

time: 308 us -> 45.1 us (0.15)
  waiting for transfers between devices: 138 us -> 0 us
  blocking collectives: 90.1 us -> 0 us
  Pallas kernels: 0 us -> 37.4 us
  starting transfers between devices: 26 us -> 0 us
  other arithmetic: 22.6 us -> 0 us
  between operations: 14.4 us -> 0.67 us
  local copies, waits for them, and re-layouts: 11.5 us -> 6.8 us
  matrix products: 4.31 us -> 0 us
    psum x1 -> x0, waiting for transfers between devices: 121 us -> none  [per_device(): coefficients = lax.psum(partial_terms, ('seg', 'bin'))]
    psum x1 -> x0, blocking collectives: 51.3 us -> none  [per_device(): totals = lax.psum(jnp.sum(smoothed, axis=1), ('seg', 'bin'))]
    all_gather x1 -> x0, blocking collectives: 38.8 us -> none  [prefix(): gathered = lax.all_gather(part, axis)]
    pallas_call x0 -> x1, Pallas kernels: none -> 37.4 us  [per_device(): pl.pallas_call(functools.partial(body, nseg, nb), out_shape=(jax.ShapeDty...]
    ppermute x6 -> x0, starting transfers between devices: 14.5 us -> none  [the longest x3 10.5 us: extended(): lax.ppermute(lax.slice_in_dim(block, block.shape[dim] - width, None, axis...]
    add x4 -> x0, other arithmetic: 12 us -> none  [the longest x2 12 us: smooth_once(): result + weight[None, :] * padded[:, tap_index:tap_index + out_width]]
    all_to_all x2 -> x0, starting transfers between devices: 11.4 us -> none  [the longest x1 6.33 us: per_device(): lax.all_to_all(target_blocks.astype(jnp.bfloat16), 'bin', split_axis=0, c...]
    all_to_all x2 -> x0, waiting for transfers between devices: 9.51 us -> none  [the longest x1 9.51 us: per_device(): lax.all_to_all(masked, 'bin', split_axis=0, concat_axis=0, tiled=True)]
  transfers between devices with their start and end apart: 9 -> 0, of which waited for: 5 -> 0; matrix products, arithmetic and copies ran while one was open for 3% -> 0% of each run, Pallas kernels for 0% -> 0%
where the time goes in v1:
time: 45.1 us; the launch traced here: 44.9 us
  Pallas kernels  37.4 us (83%)
  local copies, waits for them, and re-layouts  6.8 us (15%)
  between operations  0.67 us (1%)
    pallas_call x1, Pallas kernels, per_device(): pl.pallas_call(functools.partial(body, nseg, nb), out_shape=(jax.ShapeDty...  37.4 us
    unnamed x17, local copies, waits for them, and re-layouts  6.8 us

profile of v1, /device:TPU:0, one launch (start us, length us, event | category | flops | bytes accessed | tf_op | source)
XLA Modules:
  0.0 44.9 jit_solution(12428314429833288932)
XLA Ops:
  0.6 0.0 copy-start.6
  0.6 0.0 copy-start.5
  0.7 0.0 copy-start.4
  0.7 0.6 %copy-done.6 = s32[24]{0:T(128)S(1)} copy-done((s32[24]{0:T(128)S(1)}, s32[24]{0:T(128)}, u32[]{:S(2)}) %copy-start.6) | copy-done | bytes 120
  1.3 0.0 copy-done.5
  1.3 0.0 copy-done.4
  1.3 0.0 copy-start
  1.3 1.2 %copy-done = f32[256,1024]{1,0:T(8,128)S(1)} copy-done((f32[256,1024]{1,0:T(8,128)S(1)}, f32[256,1024]{1,0:T(8,128)}, u32[]{:S(2)}) %copy-start) | copy-done | bytes 1048600
  2.5 0.0 copy-start.1
  2.5 1.0 %copy-done.1 = f32[3,33,1024]{2,1,0:T(8,128)S(1)} copy-done((f32[3,33,1024]{2,1,0:T(8,128)S(1)}, f32[3,33,1024]{2,1,0:T(8,128)}, u32[]{:S(2)}) %copy-start.1) | copy-done | bytes 405528
  3.6 0.0 copy-start.2
  3.6 0.9 %copy-done.2 = bf16[8,128,128]{2,1,0:T(8,128)(2,1)S(1)} copy-done((bf16[8,128,128]{2,1,0:T(8,128)(2,1)S(1)}, bf16[8,128,128]{2,1,0:T(8,128)(2,1)}, u32[]{:S(2)}) %copy-start.2) | copy-done | bytes 262168
  4.5 0.0 copy-start.3
  4.5 0.7 %copy-done.3 = f32[1024]{0:T(1024)S(1)} copy-done((f32[1024]{0:T(1024)S(1)}, f32[1024]{0:T(1024)}, u32[]{:S(2)}) %copy-start.3) | copy-done | bytes 4120
  5.2 37.4 %shard_map.94 = (f32[128,256]{1,0:T(8,128)S(1)}, f32[128,1024]{1,0:T(8,128)S(1)}, f32[128,1024]{1,0:T(8,128)S(1)}) custom-call(s32[8]{0:T(128)S(1)} %copy-done.4, s32[8]{0:T(128)S(1)} %copy-done.5, s32[24]{0:T(128)S(1)} %copy-done.6, bf16[8,128,128]{2,1,0:T(8,128)(2,1)S(1)} %copy-done.2, f32[1,1024]{1,0:T(1,128)S(1)} %bitcast.1, f32[256,1024]{1,0:T(8,128)S(1)} %copy-done, ...), custom_call_target="tpu_custom_call" | custom-call | tf_op jit(solution)/shard_map/pallas_call | solution.py:371
  42.6 0.7 %copy.13 = f32[128,256]{1,0:T(8,128)} copy(f32[128,256]{1,0:T(8,128)S(1)} %get-tuple-element.6) | data formatting | bytes 262144
  43.3 0.8 %copy.14 = f32[128,1024]{1,0:T(8,128)} copy(f32[128,1024]{1,0:T(8,128)S(1)} %get-tuple-element.7) | data formatting | bytes 1048576
  44.1 0.8 %copy.15 = f32[128,1024]{1,0:T(8,128)} copy(f32[128,1024]{1,0:T(8,128)S(1)} %get-tuple-element.8) | data formatting | bytes 1048576
Async XLA Ops:
  0.6 0.7 %copy-start.6 = (s32[24]{0:T(128)S(1)}, s32[24]{0:T(128)}, u32[]{:S(2)}) copy-start(s32[24]{0:T(128)} %starts.1) | copy-start | bytes 292
  0.6 0.7 %copy-start.5 = (s32[8]{0:T(128)S(1)}, s32[8]{0:T(128)}, u32[]{:S(2)}) copy-start(s32[8]{0:T(128)} %valid.1) | copy-start | bytes 100
  0.7 0.7 %copy-start.4 = (s32[8]{0:T(128)S(1)}, s32[8]{0:T(128)}, u32[]{:S(2)}) copy-start(s32[8]{0:T(128)} %targets.1) | copy-start | bytes 100
  1.3 1.2 %copy-start = (f32[256,1024]{1,0:T(8,128)S(1)}, f32[256,1024]{1,0:T(8,128)}, u32[]{:S(2)}) copy-start(f32[256,1024]{1,0:T(8,128)} %comp.1) | copy-start | bytes 3145732
  2.5 1.0 %copy-start.1 = (f32[3,33,1024]{2,1,0:T(8,128)S(1)}, f32[3,33,1024]{2,1,0:T(8,128)}, u32[]{:S(2)}) copy-start(f32[3,33,1024]{2,1,0:T(8,128)} %kern.1) | copy-start | bytes 1216516
  3.6 0.9 %copy-start.2 = (bf16[8,128,128]{2,1,0:T(8,128)(2,1)S(1)}, bf16[8,128,128]{2,1,0:T(8,128)(2,1)}, u32[]{:S(2)}) copy-start(bf16[8,128,128]{2,1,0:T(8,128)(2,1)} %lanes.1) | copy-start | bytes 786436
  4.5 0.7 %copy-start.3 = (f32[1024]{0:T(1024)S(1)}, f32[1024]{0:T(1024)}, u32[]{:S(2)}) copy-start(f32[1024]{0:T(1024)} %param.10) | copy-start | bytes 12292

commit v2 on v1

--- a/solution.py
+++ b/solution.py
@@ -33,10 +33,11 @@
 
 
 def body(
-    nseg, nb, targets, valid, starts, lanes, panel, comp, kern,
-    coef_o, smooth_o, bridge_o,
+    nseg, nb, targets_h, valid_h, starts_h, lanes_h, panel_h, comp, kern,
+    coef_o, smooth_o, skh, skl, level_o,
+    targets, valid, starts, lanes, panel,
     send_l, recv_l, kx, taps, lrx, kh, kl, lh, ll, ah, al, bh, bl,
-    skh, skl, weights, part, gathered, c2, sums, ssem, rsem, lsem,
+    weights, part, gathered, c2, sums, ssem, rsem, lsem,
 ):
     ndev = nseg * nb
     seg, place = lax.axis_index("seg"), lax.axis_index("bin")
@@ -66,10 +67,24 @@
             barrier, inc=1, device_id=dev(lax.rem(me + hop, ndev)), device_id_type=MESH
         )
 
+    fetched = [
+        pltpu.make_async_copy(src, dst, lsem.at[i + 2])
+        for i, (src, dst) in enumerate(
+            (
+                (valid_h, valid), (targets_h, targets), (lanes_h, lanes),
+                (starts_h, starts), (panel_h, panel),
+            )
+        )
+    ]
+    for copy in fetched:
+        copy.start()
     own_k = pltpu.make_async_copy(comp, kx.at[:, pl.ds(LANES, bin_dev)], lsem.at[0])
     own_k.start()
     own_t = pltpu.make_async_copy(kern, taps.at[:, :, pl.ds(LANES, bin_dev)], lsem.at[1])
     own_t.start()
+
+    for copy in fetched:
+        copy.wait()
 
     @pl.loop(0, nb)
     def _(r):
@@ -299,41 +314,19 @@
         def _():
             wait_bytes(c2, rsem.at[8])
 
-    coef = jnp.concatenate(
+    coef_o[...] = jnp.concatenate(
         [c2[pl.ds(h * samples, samples), :] for h in range(comps // LANES)], axis=1
     )
-    coef_o[...] = coef
-    c_high, c_low = split(coef)
-    smooth_o[...] = smooth_o[...] - (
-        mm(c_high, skh[...]) + mm(c_low, skh[...]) + mm(c_high, skl[...])
-    )
-
     wait_bytes(sums.at[pl.ds(0, ndev - 1)], rsem.at[9])
-    every = jnp.sum(sums[...], axis=0)
-    part_mean = every * (1.0 / ndev)
+    part_mean = jnp.sum(sums[...], axis=0) * (1.0 / ndev)
 
     def earlier(q, acc):
         return acc + jnp.where(q < me, 1.0, 0.0) * (sums[q] - part_mean)
 
-    before_rows = lax.fori_loop(0, ndev, earlier, jnp.zeros((8, LANES), F32), unroll=ndev <= 32)
-
-    def resolve(rows):
-        level = jnp.where(eye, jnp.broadcast_to(rows[:1], (LANES, LANES)), 0.0)
-        for h in range(comps // LANES):
-            level = level - coef[:, h * LANES : (h + 1) * LANES] * rows[h + 1 : h + 2]
-        return jnp.sum(level, axis=1, keepdims=True)
-
-    mean = resolve(part_mean) * (1.0 / bin_dev)
-    carry = resolve(before_rows)
-    wide = 2 * LANES
-    ones = jnp.where(iota((wide, wide), 0) <= iota((wide, wide), 1), 1.0, 0.0).astype(BF16)
-    scale = 1.0 / math.sqrt(total_bins)
-    for m in range(bin_dev // wide):
-        window = pl.ds(m * wide, wide)
-        v_high, v_low = split(smooth_o[:, window] - mean)
-        run = mm(v_high, ones) + mm(v_low, ones) + carry
-        bridge_o[:, window] = run * scale
-        carry = run[:, wide - 1 :]
+    level_o[:8, :] = part_mean
+    level_o[8:, :] = lax.fori_loop(
+        0, ndev, earlier, jnp.zeros((8, LANES), F32), unroll=ndev <= 32
+    )
 
     wait_bytes(send_l.at[pl.ds(0, nb - 1)], ssem.at[0])
     for copy in halos + near:
@@ -354,6 +347,43 @@
             wait_bytes(part, ssem.at[7])
 
 
+def finish(total_bins, coef_i, smooth_i, skh, skl, level, coef_o, smooth_o, bridge_o):
+    samples, bin_dev = smooth_o.shape
+    comps = skh.shape[0]
+    eye = iota((LANES, LANES), 0) == iota((LANES, LANES), 1)
+    coef = coef_i[...]
+    coef_o[...] = coef
+
+    def resolve(rows):
+        level = jnp.where(eye, jnp.broadcast_to(rows[:1], (LANES, LANES)), 0.0)
+        for h in range(comps // LANES):
+            level = level - coef[:, h * LANES : (h + 1) * LANES] * rows[h + 1 : h + 2]
+        return jnp.sum(level, axis=1, keepdims=True)
+
+    mean = resolve(level[:8, :]) * (1.0 / bin_dev)
+    carry = resolve(level[8:, :])
+    c_high, c_low = split(coef)
+    wide = 2 * LANES
+    ones = jnp.where(iota((wide, wide), 0) <= iota((wide, wide), 1), 1.0, 0.0).astype(BF16)
+    scale = 1.0 / math.sqrt(total_bins)
+    runs = []
+    for m in range(bin_dev // wide):
+        window = pl.ds(m * wide, wide)
+        value = smooth_i[:, window] - (
+            mm(c_high, skh[:, window]) + mm(c_low, skh[:, window]) + mm(c_high, skl[:, window])
+        )
+        smooth_o[:, window] = value
+        v_high, v_low = split(value - mean)
+        runs.append(mm(v_high, ones) + mm(v_low, ones))
+    for m, run in enumerate(runs):
+        bridge_o[:, pl.ds(m * wide, wide)] = (run + carry) * scale
+        carry = carry + run[:, wide - 1 :]
+
+
+def in_hbm(x):
+    return pltpu.with_memory_space_constraint(x, pltpu.HBM)
+
+
 def solution(mesh):
     nseg, nb = mesh.shape["seg"], mesh.shape["bin"]
     ndev = nseg * nb
@@ -366,18 +396,25 @@
         bands = 3 * (bin_dev // LANES) + 2
         vmem, smem = pltpu.VMEM, pltpu.SMEM
         whole = pl.BlockSpec(memory_space=vmem)
-        scalar = pl.BlockSpec(memory_space=smem)
-        away = pl.BlockSpec(memory_space=pl.ANY)
-        return pl.pallas_call(
+        away = pl.BlockSpec(memory_space=pltpu.HBM)
+        sds = jax.ShapeDtypeStruct
+        coef, smooth, skh, skl, level = pl.pallas_call(
             functools.partial(body, nseg, nb),
             out_shape=(
-                jax.ShapeDtypeStruct((samples, comps), F32),
-                jax.ShapeDtypeStruct((samples, bin_dev), F32),
-                jax.ShapeDtypeStruct((samples, bin_dev), F32),
+                sds((samples, comps), F32),
+                sds((samples, bin_dev), F32),
+                sds((comps, bin_dev), BF16),
+                sds((comps, bin_dev), BF16),
+                sds((16, LANES), F32),
             ),
-            in_specs=[scalar, scalar, scalar, whole, whole, away, away],
-            out_specs=(whole, whole, whole),
+            in_specs=[away] * 7,
+            out_specs=(whole,) * 5,
             scratch_shapes=[
+                smem(targets.shape, jnp.int32),
+                smem(valid.shape, jnp.int32),
+                smem(starts.shape, jnp.int32),
+                vmem(lanes.shape, BF16),
+                vmem((1, bin_dev), F32),
                 vmem((nb, samples + 16, LANES), BF16),
                 vmem((nb, samples + 16, LANES), BF16),
                 vmem((comps, ext), F32),
@@ -391,8 +428,6 @@
                 vmem((comps, ext), BF16),
                 vmem((comps, ext), BF16),
                 vmem((comps, ext), BF16),
-                vmem((comps, bin_dev), BF16),
-                vmem((comps, bin_dev), BF16),
                 vmem((bands, 2 * LANES, 2 * LANES), BF16),
                 vmem((samples * comps // LANES, LANES), F32),
                 vmem((ndev, 8, LANES), F32),
@@ -400,12 +435,23 @@
                 vmem((ndev, 8, LANES), F32),
                 pltpu.SemaphoreType.DMA((10,)),
                 pltpu.SemaphoreType.DMA((10,)),
-                pltpu.SemaphoreType.DMA((2,)),
+                pltpu.SemaphoreType.DMA((7,)),
             ],
             compiler_params=pltpu.CompilerParams(
-                collective_id=0, has_side_effects=True, vmem_limit_bytes=48 << 20
+                collective_id=0, has_side_effects=True, vmem_limit_bytes=40 << 20
             ),
-        )(targets, valid, starts, lanes, panel.reshape(1, bin_dev), comp, kern)
+        )(*map(in_hbm, (targets, valid, starts, lanes, panel.reshape(1, bin_dev), comp, kern)))
+        return pl.pallas_call(
+            functools.partial(finish, bin_dev * ndev),
+            out_shape=(
+                sds((samples, comps), F32),
+                sds((samples, bin_dev), F32),
+                sds((samples, bin_dev), F32),
+            ),
+            in_specs=[whole] * 5,
+            out_specs=(whole,) * 3,
+            compiler_params=pltpu.CompilerParams(vmem_limit_bytes=16 << 20),
+        )(coef, smooth, skh, skl, level)
 
     in_specs = (
         P(("seg", "bin"), None, None),

time: 45.1 us -> 39.2 us (0.87)
  local copies, waits for them, and re-layouts: 6.8 us -> 0 us
  Pallas kernels: 37.4 us -> 38.4 us
    unnamed x17 -> x0, local copies, waits for them, and re-layouts: 6.8 us -> none
    pallas_call x1 -> x2, Pallas kernels: 37.4 us -> 38.4 us  [the longest x1 36.4 us: per_device(): pl.pallas_call(functools.partial(body, nseg, nb), out_shape=(sds((samples...]
where the time goes in v2:
time: 39.2 us; the launch traced here: 39 us
  Pallas kernels  38.4 us (98%)
  between operations  0.64 us (2%)
    pallas_call x1, Pallas kernels, per_device(): pl.pallas_call(functools.partial(body, nseg, nb), out_shape=(sds((samples...  36.4 us
    pallas_call x1, Pallas kernels, per_device(): pl.pallas_call(functools.partial(finish, bin_dev * ndev), out_shape=(sds(...  2.01 us

profile of v2, /device:TPU:0, one launch (start us, length us, event | category | flops | bytes accessed | tf_op | source)
XLA Modules:
  0.0 39.0 jit_solution(3512613592555452126)
XLA Ops:
  0.6 36.4 %shard_map.94 = (f32[128,256]{1,0:T(8,128)S(1)}, f32[128,1024]{1,0:T(8,128)S(1)}, bf16[256,1024]{1,0:T(8,128)(2,1)S(1)}, bf16[256,1024]{1,0:T(8,128)(2,1)S(1)}, f32[16,128]{1,0:T(8,128)S(1)}) custom-call(s32[8]{0:T(128)} %targets_h.1, s32[8]{0:T(128)} %valid_h.1, s32[24]{0:T(128)} %starts_h.1, bf16[8,128,128]{2,1,0:T(8,128)(2,1)} %lanes_h.1, ...), custom_call_target="tpu_custom_call" | custom-call | tf_op jit(solution)/shard_map/pallas_call | solution.py:401
  37.0 2.0 %shard_map.95 = (f32[128,256]{1,0:T(8,128)}, f32[128,1024]{1,0:T(8,128)}, f32[128,1024]{1,0:T(8,128)}) custom-call(f32[128,256]{1,0:T(8,128)S(1)} %get-tuple-element.8.coef_i, f32[128,1024]{1,0:T(8,128)S(1)} %get-tuple-element.9.smooth_i, bf16[256,1024]{1,0:T(8,128)(2,1)S(1)} %get-tuple-element.10.skh, bf16[256,1024]{1,0:T(8,128)(2,1)S(1)} %get-tuple-element.11.skl, ...), custom_call_target="tpu_custom_call" | custom-call | tf_op jit(solution)/shard_map/pallas_call | solution.py:444

commit v3 on v2

--- a/solution.py
+++ b/solution.py
@@ -37,7 +37,7 @@
     coef_o, smooth_o, skh, skl, level_o,
     targets, valid, starts, lanes, panel,
     send_l, recv_l, kx, taps, lrx, kh, kl, lh, ll, ah, al, bh, bl,
-    weights, part, gathered, c2, sums, ssem, rsem, lsem,
+    weights, part, gathered, crossed, c2, sums, kout, kin, ssem, rsem, lsem,
 ):
     ndev = nseg * nb
     seg, place = lax.axis_index("seg"), lax.axis_index("bin")
@@ -61,11 +61,28 @@
 
     barrier = pltpu.get_barrier_semaphore()
 
-    @pl.loop(1, ndev)
-    def _(hop):
-        pl.semaphore_signal(
-            barrier, inc=1, device_id=dev(lax.rem(me + hop, ndev)), device_id_type=MESH
-        )
+    def each(start, stop, do):
+        if stop - start <= 8:
+            for hop in range(start, stop):
+                do(hop)
+        else:
+            pl.loop(start, stop)(do)
+
+    def bin_peer(hop):
+        return (seg, lax.rem(place + hop, nb))
+
+    def seg_peer(hop):
+        return (lax.rem(seg + hop, nseg), place)
+
+    right, left = dev(lax.rem(me + 1, ndev)), dev(lax.rem(me + ndev - 1, ndev))
+
+    def greet(device):
+        pl.semaphore_signal(barrier, inc=1, device_id=device, device_id_type=MESH)
+
+    each(1, nb, lambda hop: greet(bin_peer(hop)))
+    each(1, nseg, lambda hop: greet(seg_peer(hop)))
+    greet(right)
+    greet(left)
 
     fetched = [
         pltpu.make_async_copy(src, dst, lsem.at[i + 2])
@@ -93,23 +110,33 @@
         mark = jnp.full((16, LANES), targets[r], jnp.int32).astype(F32)
         send_l[r, samples:, :] = mark.astype(BF16)
 
-    pl.semaphore_wait(barrier, ndev - 1)
-
-    @pl.loop(1, nb)
-    def _(hop):
-        to = lax.rem(place + hop, nb)
-        remote(send_l.at[to], recv_l.at[place], 0, (seg, to)).start()
-
-    right, left = dev(lax.rem(me + 1, ndev)), dev(lax.rem(me + ndev - 1, ndev))
+    pl.semaphore_wait(barrier, nb + nseg)
+
+    def exchange(hop):
+        to = bin_peer(hop)
+        remote(send_l.at[to[1]], recv_l.at[place], 0, to).start()
+
+    each(1, nb, exchange)
     low, high = pl.ds(0, LANES), pl.ds(bin_dev + LANES, LANES)
     head, tail = pl.ds(0, LANES), pl.ds(bin_dev - LANES, LANES)
     halos = [
         remote(kern.at[pl.ds(0, 2), :, tail], taps.at[pl.ds(0, 2), :, low], 1, right),
         remote(kern.at[pl.ds(0, 2), :, head], taps.at[pl.ds(0, 2), :, high], 2, left),
-        remote(comp.at[:, tail], kx.at[:, low], 3, right),
-        remote(comp.at[:, head], kx.at[:, high], 4, left),
+        remote(kout.at[0], kin.at[0], 3, right),
+        remote(kout.at[1], kin.at[1], 4, left),
     ]
-    for copy in halos:
+    for copy in halos[:2]:
+        copy.start()
+    own_k.wait()
+    lower_half = iota((LANES, LANES), 1) < LANES // 2
+    first_block, last_block = pl.ds(LANES, LANES), pl.ds(bin_dev, LANES)
+    kout[0] = jnp.where(
+        lower_half, pltpu.roll(kx[LANES:, last_block], LANES // 2, 1), kx[:LANES, last_block]
+    )
+    kout[1] = jnp.where(
+        lower_half, kx[:LANES, first_block], pltpu.roll(kx[LANES:, first_block], LANES // 2, 1)
+    )
+    for copy in halos[2:]:
         copy.start()
 
     recv_l[place] = send_l[place]
@@ -183,11 +210,13 @@
             src_low[:, window], weights[base + m, :, :LANES]
         )
 
-    def smooth(src, mid, end, rows, store):
-        for m in range(blocks + 1):
+    def smooth_first(src, mid, rows, which):
+        for m in which:
             out = split(smooth_pass(src[0], src[1], m, plan[0][3]))
             for ref, value in zip(mid, out):
                 ref[:rows, pl.ds(m * LANES, LANES)] = value
+
+    def smooth_rest(mid, end, rows, store):
         for m in range(blocks + 1):
             out = split(
                 smooth_pass(mid[0].at[:rows], mid[1].at[:rows], m, plan[1][3])
@@ -206,18 +235,15 @@
     def as_row(column):
         return jnp.sum(jnp.where(eye, column, 0.0), axis=0, keepdims=True)
 
-    own_k.wait()
-    halos[2].wait_recv()
-    halos[3].wait_recv()
+    own = pl.ds(LANES, bin_dev)
     for ref in (ah, al, bh, bl):
         ref[:, pl.ds(bin_dev + LANES, LANES)] = jnp.zeros((comps, LANES), BF16)
-    kh[...], kl[...] = split(kx[...])
+    kh[:, own], kl[:, own] = split(kx[:, own])
+    smooth_first((kh, kl), (ah, al), comps, range(1, blocks))
 
     def store_k(m, out):
         window = pl.ds(m * LANES, LANES)
         skh[:, window], skl[:, window] = split(out)
-
-    k_total = smooth((kh, kl), (ah, al), (bh, bl), comps, store_k)
 
     wait_bytes(recv_l.at[pl.ds(0, nb - 1)], rsem.at[0])
     for b in range(blocks):
@@ -240,7 +266,6 @@
     for copy in near:
         copy.start()
 
-    own = pl.ds(LANES, bin_dev)
     lh[:, own], ll[:, own] = split(lrx[:, own])
     terms = (
         mm(lh[:, own], kh[:, own], (1, 1))
@@ -250,23 +275,52 @@
     for h in range(comps // LANES):
         part[pl.ds(h * samples, samples), :] = terms[:, h * LANES : (h + 1) * LANES]
 
-    tiles = part.shape[0] // 8
-    stride = ndev // tiles
-    mine = lax.div(me, stride)
-    owner = lax.rem(me, stride) == 0
-
-    def tile(j):
-        return pl.ds(pl.multiple_of(j * 8, 8), 8)
-
-    @pl.loop(1 if stride == 1 else 0, tiles)
-    def _(hop):
-        j = lax.rem(mine + hop, tiles)
-        copy = remote(part.at[tile(j)], gathered.at[me], 7, dev(j * stride))
+    rows = max(8, part.shape[0] // nb)
+    chunks = part.shape[0] // rows
+    stride = nb // chunks
+    mine = lax.div(place, stride)
+    owner = lax.rem(place, stride) == 0
+
+    def chunk(j):
+        return pl.ds(pl.multiple_of(j * rows, 8), rows)
+
+    def on_owner(do):
+        if stride == 1:
+            do()
+        else:
+            pl.when(owner)(do)
+
+    def off_owner(do):
+        if stride > 1:
+            pl.when(jnp.logical_not(owner))(do)
+
+    def spread(hop):
+        j = lax.rem(mine + hop, chunks)
+        copy = remote(part.at[chunk(j)], gathered.at[place], 7, (seg, j * stride))
         if stride == 1:
             copy.start()
         else:
-            pl.when(j * stride != me)(copy.start)
-
+            pl.when(j * stride != place)(copy.start)
+
+    each(1 if stride == 1 else 0, chunks, spread)
+
+    halos[2].wait_recv()
+    halos[3].wait_recv()
+    for side, edge in enumerate((low, high)):
+        kh[:LANES, edge], kl[:LANES, edge] = split(kin[side])
+        kh[LANES:, edge], kl[LANES:, edge] = split(pltpu.roll(kin[side], LANES // 2, 1))
+    smooth_first((kh, kl), (ah, al), comps, (0, blocks))
+    k_total = smooth_rest((ah, al), (bh, bl), comps, store_k)
+
+    def reduce_and_cross():
+        gathered[place] = part[chunk(mine), :]
+        wait_bytes(gathered.at[pl.ds(0, nb - 1)], rsem.at[7])
+        crossed[seg] = jnp.sum(gathered[...], axis=0)
+        each(1, nseg, lambda hop: remote(
+            crossed.at[seg], crossed.at[seg], 10, seg_peer(hop)
+        ).start())
+
+    on_owner(reduce_and_cross)
     for copy in near:
         copy.wait_recv()
     for edge in (low, high):
@@ -275,49 +329,35 @@
     def store_l(m, out):
         smooth_o[:, pl.ds(m * LANES, LANES)] = out
 
-    l_total = smooth((lh, ll), (ah, al), (bh, bl), samples, store_l)
+    smooth_first((lh, ll), (ah, al), samples, range(blocks + 1))
+    l_total = smooth_rest((ah, al), (bh, bl), samples, store_l)
     sums[me] = jnp.concatenate(
         [as_row(l_total)]
         + [as_row(k_total[h * LANES : (h + 1) * LANES]) for h in range(comps // LANES)]
         + [jnp.zeros((7 - comps // LANES, LANES), F32)],
         axis=0,
     )
-
-    def reduce_and_send():
-        gathered[me] = part[tile(mine), :]
-        wait_bytes(gathered.at[pl.ds(0, ndev - 1)], rsem.at[7])
-        c2[tile(mine), :] = jnp.sum(gathered[...], axis=0)
-
-        @pl.loop(1, ndev)
-        def _(hop):
-            to = dev(lax.rem(me + hop, ndev))
-            remote(c2.at[tile(mine)], c2.at[tile(mine)], 8, to).start()
-
-    if stride == 1:
-        reduce_and_send()
-    else:
-        pl.when(owner)(reduce_and_send)
-
-    @pl.loop(1, ndev)
-    def _(hop):
-        remote(sums.at[me], sums.at[me], 9, dev(lax.rem(me + hop, ndev))).start()
-
-    if stride == 1:
-        wait_bytes(c2.at[pl.ds(0, 8 * (tiles - 1))], rsem.at[8])
-    else:
-
-        @pl.when(owner)
-        def _():
-            wait_bytes(c2.at[pl.ds(0, 8 * (tiles - 1))], rsem.at[8])
-
-        @pl.when(jnp.logical_not(owner))
-        def _():
-            wait_bytes(c2, rsem.at[8])
-
+    each(1, nb, lambda hop: remote(sums.at[me], sums.at[me], 9, bin_peer(hop)).start())
+
+    def add_and_return():
+        wait_bytes(crossed.at[pl.ds(0, nseg - 1)], rsem.at[10])
+        c2[chunk(mine), :] = jnp.sum(crossed[...], axis=0)
+        each(1, nb, lambda hop: remote(
+            c2.at[chunk(mine)], c2.at[chunk(mine)], 8, bin_peer(hop)
+        ).start())
+
+    on_owner(add_and_return)
+    wait_bytes(sums.at[pl.ds(0, nb - 1)], rsem.at[9])
+    stretch = pl.ds(pl.multiple_of(seg * nb, nb), nb)
+    each(1, nseg, lambda hop: remote(
+        sums.at[stretch], sums.at[stretch], 11, seg_peer(hop)
+    ).start())
+    on_owner(lambda: wait_bytes(c2.at[pl.ds(0, rows * (chunks - 1))], rsem.at[8]))
+    off_owner(lambda: wait_bytes(c2, rsem.at[8]))
     coef_o[...] = jnp.concatenate(
         [c2[pl.ds(h * samples, samples), :] for h in range(comps // LANES)], axis=1
     )
-    wait_bytes(sums.at[pl.ds(0, ndev - 1)], rsem.at[9])
+    wait_bytes(sums.at[pl.ds(0, ndev - nb)], rsem.at[11])
     part_mean = jnp.sum(sums[...], axis=0) * (1.0 / ndev)
 
     def earlier(q, acc):
@@ -331,20 +371,16 @@
     wait_bytes(send_l.at[pl.ds(0, nb - 1)], ssem.at[0])
     for copy in halos + near:
         copy.wait_send()
-    wait_bytes(sums.at[pl.ds(0, ndev - 1)], ssem.at[9])
-    if stride == 1:
-        wait_bytes(part.at[pl.ds(0, 8 * (tiles - 1))], ssem.at[7])
-        wait_bytes(gathered.at[pl.ds(0, ndev - 1)], ssem.at[8])
-    else:
-
-        @pl.when(owner)
-        def _():
-            wait_bytes(part.at[pl.ds(0, 8 * (tiles - 1))], ssem.at[7])
-            wait_bytes(gathered.at[pl.ds(0, ndev - 1)], ssem.at[8])
-
-        @pl.when(jnp.logical_not(owner))
-        def _():
-            wait_bytes(part, ssem.at[7])
+    wait_bytes(sums.at[pl.ds(0, nb - 1)], ssem.at[9])
+    wait_bytes(sums.at[pl.ds(0, ndev - nb)], ssem.at[11])
+
+    def drain():
+        wait_bytes(part.at[pl.ds(0, rows * (chunks - 1))], ssem.at[7])
+        wait_bytes(gathered.at[pl.ds(0, nb - 1)], ssem.at[8])
+        wait_bytes(crossed.at[pl.ds(0, nseg - 1)], ssem.at[10])
+
+    on_owner(drain)
+    off_owner(lambda: wait_bytes(part, ssem.at[7]))
 
 
 def finish(total_bins, coef_i, smooth_i, skh, skl, level, coef_o, smooth_o, bridge_o):
@@ -393,6 +429,7 @@
         comps, bin_dev = comp.shape
         layers, ntaps = kern.shape[:2]
         ext = bin_dev + 2 * LANES
+        flat = samples * comps // LANES
         bands = 3 * (bin_dev // LANES) + 2
         vmem, smem = pltpu.VMEM, pltpu.SMEM
         whole = pl.BlockSpec(memory_space=vmem)
@@ -429,12 +466,15 @@
                 vmem((comps, ext), BF16),
                 vmem((comps, ext), BF16),
                 vmem((bands, 2 * LANES, 2 * LANES), BF16),
-                vmem((samples * comps // LANES, LANES), F32),
+                vmem((flat, LANES), F32),
+                vmem((nb, max(8, flat // nb), LANES), F32),
+                vmem((nseg, max(8, flat // nb), LANES), F32),
+                vmem((flat, LANES), F32),
                 vmem((ndev, 8, LANES), F32),
-                vmem((samples * comps // LANES, LANES), F32),
-                vmem((ndev, 8, LANES), F32),
-                pltpu.SemaphoreType.DMA((10,)),
-                pltpu.SemaphoreType.DMA((10,)),
+                vmem((2, LANES, LANES), F32),
+                vmem((2, LANES, LANES), F32),
+                pltpu.SemaphoreType.DMA((12,)),
+                pltpu.SemaphoreType.DMA((12,)),
                 pltpu.SemaphoreType.DMA((7,)),
             ],
             compiler_params=pltpu.CompilerParams(

time: 39.2 us -> 35.9 us (0.916)
  Pallas kernels: 38.4 us -> 35.1 us
    pallas_call x1, Pallas kernels: 36.4 us -> 33.1 us  [per_device(): pl.pallas_call(functools.partial(body, nseg, nb), out_shape=(sds((samples...]
where the time goes in v3:
time: 35.9 us; the launch traced here: 35.7 us
  Pallas kernels  35.1 us (98%)
  between operations  0.64 us (2%)
    pallas_call x1, Pallas kernels, per_device(): pl.pallas_call(functools.partial(body, nseg, nb), out_shape=(sds((samples...  33.1 us
    pallas_call x1, Pallas kernels, per_device(): pl.pallas_call(functools.partial(finish, bin_dev * ndev), out_shape=(sds(...  2.01 us

profile of v3, /device:TPU:0, one launch (start us, length us, event | category | flops | bytes accessed | tf_op | source)
XLA Modules:
  0.0 35.7 jit_solution(900489240958511255)
XLA Ops:
  0.6 33.1 %shard_map.94 = (f32[128,256]{1,0:T(8,128)S(1)}, f32[128,1024]{1,0:T(8,128)S(1)}, bf16[256,1024]{1,0:T(8,128)(2,1)S(1)}, bf16[256,1024]{1,0:T(8,128)(2,1)S(1)}, f32[16,128]{1,0:T(8,128)S(1)}) custom-call(s32[8]{0:T(128)} %targets_h.1, s32[8]{0:T(128)} %valid_h.1, s32[24]{0:T(128)} %starts_h.1, bf16[8,128,128]{2,1,0:T(8,128)(2,1)} %lanes_h.1, ...), custom_call_target="tpu_custom_call" | custom-call | tf_op jit(solution)/shard_map/pallas_call | solution.py:438
  33.7 2.0 %shard_map.95 = (f32[128,256]{1,0:T(8,128)}, f32[128,1024]{1,0:T(8,128)}, f32[128,1024]{1,0:T(8,128)}) custom-call(f32[128,256]{1,0:T(8,128)S(1)} %get-tuple-element.8.coef_i, f32[128,1024]{1,0:T(8,128)S(1)} %get-tuple-element.9.smooth_i, bf16[256,1024]{1,0:T(8,128)(2,1)S(1)} %get-tuple-element.10.skh, bf16[256,1024]{1,0:T(8,128)(2,1)S(1)} %get-tuple-element.11.skl, ...), custom_call_target="tpu_custom_call" | custom-call | tf_op jit(solution)/shard_map/pallas_call | solution.py:484

commit v4 on v3

--- a/solution.py
+++ b/solution.py
@@ -100,15 +100,18 @@
     own_t = pltpu.make_async_copy(kern, taps.at[:, :, pl.ds(LANES, bin_dev)], lsem.at[1])
     own_t.start()
 
-    for copy in fetched:
+    for copy in fetched[:3]:
         copy.wait()
 
-    @pl.loop(0, nb)
-    def _(r):
+    def mask(r):
         keep = iota((samples, LANES), 1) < valid[r]
         send_l[r, :samples, :] = jnp.where(keep, lanes[r].astype(F32), 0.0).astype(BF16)
         mark = jnp.full((16, LANES), targets[r], jnp.int32).astype(F32)
         send_l[r, samples:, :] = mark.astype(BF16)
+
+    each(0, nb, mask)
+    for copy in fetched[3:]:
+        copy.wait()
 
     pl.semaphore_wait(barrier, nb + nseg)
 

time: 35.9 us -> 35.9 us (level)
  no operation moved by 1% of the time
where the time goes in v4:
time: 35.9 us; the launch traced here: 35.7 us
  Pallas kernels  35.1 us (98%)
  between operations  0.64 us (2%)
    pallas_call x1, Pallas kernels, per_device(): pl.pallas_call(functools.partial(body, nseg, nb), out_shape=(sds((samples...  33.1 us
    pallas_call x1, Pallas kernels, per_device(): pl.pallas_call(functools.partial(finish, bin_dev * ndev), out_shape=(sds(...  2.01 us

profile of v4, /device:TPU:0, one launch (start us, length us, event | category | flops | bytes accessed | tf_op | source)
XLA Modules:
  0.0 35.7 jit_solution(14498233887964743152)
XLA Ops:
  0.6 33.1 %shard_map.94 = (f32[128,256]{1,0:T(8,128)S(1)}, f32[128,1024]{1,0:T(8,128)S(1)}, bf16[256,1024]{1,0:T(8,128)(2,1)S(1)}, bf16[256,1024]{1,0:T(8,128)(2,1)S(1)}, f32[16,128]{1,0:T(8,128)S(1)}) custom-call(s32[8]{0:T(128)} %targets_h.1, s32[8]{0:T(128)} %valid_h.1, s32[24]{0:T(128)} %starts_h.1, bf16[8,128,128]{2,1,0:T(8,128)(2,1)} %lanes_h.1, ...), custom_call_target="tpu_custom_call" | custom-call | tf_op jit(solution)/shard_map/pallas_call | solution.py:441
  33.7 2.0 %shard_map.95 = (f32[128,256]{1,0:T(8,128)}, f32[128,1024]{1,0:T(8,128)}, f32[128,1024]{1,0:T(8,128)}) custom-call(f32[128,256]{1,0:T(8,128)S(1)} %get-tuple-element.8.coef_i, f32[128,1024]{1,0:T(8,128)S(1)} %get-tuple-element.9.smooth_i, bf16[256,1024]{1,0:T(8,128)(2,1)S(1)} %get-tuple-element.10.skh, bf16[256,1024]{1,0:T(8,128)(2,1)S(1)} %get-tuple-element.11.skl, ...), custom_call_target="tpu_custom_call" | custom-call | tf_op jit(solution)/shard_map/pallas_call | solution.py:487
